TPU v7x, 32 devices: a whole 2x2x4 slice. The times are simulated.
32 devices in a mesh: wave: 16 (over z, y, x), field: 2 (over core).
Axes of the slice: x: 2, y: 2, z: 4, core: 2. Of those that a mesh axis runs over, the one named last changes fastest.
Arguments:
- right_vector: float32 [4, 3, 512, 2, 512], P('field', None, 'wave'), may hold values from -8 to 8
- left_prev: float32 [4, 3, 512, 2, 512], P('field', None, 'wave'), may hold values from -6 to 6
- beta_prev: float32 [1], replicated, may hold values from 0.5 to 2
- kept_vectors: bfloat16 [20, 4, 3, 512, 2, 512], P(None, 'field', None, 'wave'), may hold values from -8 to 8
- kept_count: int32 [1], replicated, may hold values from 1 to 20
- wave_table: int32 [512], replicated, may hold values from 0 to 511, each once
- legendre: float32 [512, 512, 512], P('wave'), may hold values from -0.25 to 0.25
- quad_weights: float32 [512], replicated, may hold values from 0.2 to 1
- coef_value: bfloat16 [3, 3, 512, 1024], P(None, None, 'wave'), may hold values from -2.390625 to 2.390625
- coef_zonal: bfloat16 [3, 3, 512, 1024], P(None, None, 'wave'), may hold values from -2.390625 to 2.390625
Outputs:
- left_vector: float32 [4, 3, 512, 2, 512], P('field', None, 'wave')
- right_next: float32 [4, 3, 512, 2, 512], P('field', None, 'wave')
- correlations: float32 [20], replicated
- norms: float32 [2], replicated
Inputs may be any that keep to these rules, and one draw needn't show every extreme that they name: The stored vectors numbered below kept_count take part. A permutation: spectral slot s holds zonal wavenumber wave_table[s].
All inputs are finite; a program needn't handle non-finite values.
Results may differ from a plain program's by a relative error of at most 0.0003.
Values sent between devices are 32-bit elements; how exact they have to be, the bound alone decides.
A program may use at most 192 MiB of HBM per device.

v0:
```python
import math
import jax
import jax.numpy as jnp
from jax import lax
from jax.sharding import PartitionSpec as P

time_step = 0.5
epsilon = 1e-06
highest = lax.Precision.HIGHEST


def fourier_tables(wave_table, longitudes, wave_count):
    column = jnp.arange(longitudes, dtype=jnp.int32)
    phase_index = wave_table[:, None] * column[None, :] % longitudes
    angle_rows = phase_index.astype(jnp.float32) * (2.0 * math.pi / longitudes)
    cosine = jnp.cos(angle_rows)
    sine_rows = jnp.sin(angle_rows)
    factor = wave_count ** (-0.5)
    slope_scale = (wave_table.astype(jnp.float32) / wave_count * factor)[:, None, None]
    value_rows = jnp.stack([cosine, -sine_rows], axis=1) * factor
    slope_rows = jnp.stack([-sine_rows, -cosine], axis=1) * slope_scale
    synthesis = jnp.stack([value_rows, slope_rows], axis=2)
    analysis = jnp.stack([cosine, -sine_rows], axis=1) * longitudes ** (-0.5)
    return (synthesis, analysis)


def body(
    right_vector,
    left_prev,
    beta_prev,
    kept_vectors,
    kept_count,
    wave_table,
    legendre,
    quad_weights,
    coef_value,
    coef_zonal,
):
    levels = right_vector.shape[0]
    fields = right_vector.shape[1]
    waves_dev = legendre.shape[0]
    degrees = legendre.shape[1]
    lat_dev = coef_value.shape[2]
    longitudes = coef_value.shape[3]
    groups = lax.axis_size("wave")
    keep_count = kept_vectors.shape[0]
    entries = float(right_vector.size * groups * lax.axis_size("field"))
    device = lax.axis_index("wave")
    own_waves = lax.dynamic_slice_in_dim(wave_table, device * waves_dev, waves_dev)
    degree_ids = jnp.arange(degrees, dtype=jnp.int32)
    live_mask = (degree_ids[None, :] >= own_waves[:, None]).astype(jnp.float32)
    wide_mask = live_mask[None, None, :, None, :]
    own_weights = lax.dynamic_slice_in_dim(quad_weights, device * lat_dev, lat_dev)[
        None, None, :, None
    ]
    synthesis, analysis = fourier_tables(wave_table, longitudes, degrees)
    synthesis = synthesis.reshape(groups, waves_dev, 2, 2, longitudes)
    analysis = analysis.reshape(groups, waves_dev, 2, longitudes)
    blocked = legendre.reshape(waves_dev, degrees, groups, lat_dev)
    value_coef = coef_value.astype(jnp.float32)
    zonal_coef = coef_zonal.astype(jnp.float32)

    def to_latitudes(spectral):
        latitude_part = jnp.einsum("lfsrn,snwt->lwftsr", spectral, blocked, precision=highest)
        return latitude_part.reshape(levels, groups, fields * lat_dev * waves_dev * 2)

    def to_degrees(gathered):
        spectral = jnp.einsum("lwftsr,snwt->lfsrn", gathered, blocked, precision=highest)
        return spectral * wide_mask

    right_live = right_vector * wide_mask
    prev_live = left_prev * wide_mask
    block_in = lax.all_to_all(
        to_latitudes(right_live), "wave", split_axis=1, concat_axis=1, tiled=True
    )
    item_count = block_in.shape[0]
    spread = block_in.reshape(item_count, groups, fields, lat_dev, waves_dev, 2)
    grid_values = jnp.einsum("iwftsr,wsrkx->ikftx", spread, synthesis, precision=highest)
    tendency = jnp.sum(value_coef[None] * grid_values[:, 0, None], axis=2)
    tendency = tendency + jnp.sum(zonal_coef[None] * grid_values[:, 1, None], axis=2)
    weighted = tendency * own_weights
    outgoing = jnp.einsum("iftx,wsrx->iwftsr", weighted, analysis, precision=highest)
    returned = lax.all_to_all(
        outgoing.reshape(item_count, groups, -1), "wave", split_axis=1, concat_axis=1, tiled=True
    )
    gathered = returned.reshape(item_count, groups, fields, lat_dev, waves_dev, 2)
    residual_left = right_live + time_step * to_degrees(gathered) - beta_prev[0] * prev_live
    kept_live = (kept_vectors.astype(jnp.float32) * wide_mask[None]).reshape(keep_count, -1)
    live_flags = (jnp.arange(keep_count, dtype=jnp.int32) < kept_count[0]).astype(jnp.float32)

    def project(vector):
        return jnp.dot(kept_live, vector.reshape(-1), precision=highest)

    block_in = lax.all_to_all(
        to_latitudes(residual_left), "wave", split_axis=1, concat_axis=1, tiled=True
    )
    item_count = block_in.shape[0]
    spread = block_in.reshape(item_count, groups, fields, lat_dev, waves_dev, 2)
    weighted = jnp.einsum("iwftsr,wsrx->iftx", spread, analysis, precision=highest) * own_weights
    value_part = jnp.sum(value_coef[None] * weighted[:, :, None], axis=1)
    zonal_part = jnp.sum(zonal_coef[None] * weighted[:, :, None], axis=1)
    stacked = jnp.stack([value_part, zonal_part], axis=1)
    outgoing = jnp.einsum("ikftx,wsrkx->iwftsr", stacked, synthesis, precision=highest)
    returned = lax.all_to_all(
        outgoing.reshape(item_count, groups, -1), "wave", split_axis=1, concat_axis=1, tiled=True
    )
    gathered = returned.reshape(item_count, groups, fields, lat_dev, waves_dev, 2)
    adjoint_raw = residual_left + time_step * to_degrees(gathered)
    totals = lax.psum(
        (
            jnp.sum(residual_left * residual_left),
            jnp.sum(adjoint_raw * adjoint_raw),
            jnp.sum(adjoint_raw * right_live),
            jnp.sum(right_live * right_live),
            project(adjoint_raw),
            project(right_live),
            jnp.dot(kept_live, kept_live.T, precision=highest),
        ),
        ("wave", "field"),
    )
    left_square, image_square, image_cross, right_square, kept_image, kept_right, gram_matrix = [
        summed / entries for summed in totals
    ]
    alpha_norm = jnp.sqrt(left_square + epsilon)
    left_vector = residual_left / alpha_norm
    raw_correlation = kept_image / alpha_norm - alpha_norm * kept_right
    correlations = raw_correlation * live_flags
    square = (
        image_square / (alpha_norm * alpha_norm)
        - 2.0 * image_cross
        + alpha_norm * alpha_norm * right_square
    )
    square = (
        square
        - 2.0 * jnp.sum(correlations * raw_correlation)
        + jnp.dot(
            correlations, jnp.dot(gram_matrix, correlations, precision=highest), precision=highest
        )
    )
    beta_norm = jnp.sqrt(square + epsilon)
    orthogonal = (
        adjoint_raw / alpha_norm
        - alpha_norm * right_live
        - jnp.dot(correlations, kept_live, precision=highest).reshape(right_live.shape)
    )
    return (left_vector, orthogonal / beta_norm, correlations, jnp.stack([alpha_norm, beta_norm]))


def solution(mesh):
    return jax.shard_map(
        body,
        mesh=mesh,
        in_specs=(
            P("field", None, "wave", None, None),
            P("field", None, "wave", None, None),
            P(),
            P(None, "field", None, "wave", None, None),
            P(),
            P(),
            P("wave", None, None),
            P(),
            P(None, None, "wave", None),
            P(None, None, "wave", None),
        ),
        out_specs=(
            P("field", None, "wave", None, None),
            P("field", None, "wave", None, None),
            P(),
            P(),
        ),
        check_vma=False,
    )
```

profile of v0, /device:TPU:0, one launch (start us, length us, event | category | flops | bytes accessed | tf_op | source)
XLA Modules:
  0.0 760.5 jit_solution(3930852589484011653)
XLA Ops:
  0.6 0.8 dynamic_slice.6
  1.4 0.1 fusion.74
  1.5 33.4 %copy.73 = f32[32,512,512]{1,2,0:T(8,128)} copy(f32[32,512,512]{2,1,0:T(8,128)} %param.16) | data formatting | bytes 67108864 | tf_op args[6]
  34.9 86.2 %convolution_bitcast_fusion.1 = f32[2,16,3,32,32,2]{3,2,1,5,0,4:T(4,128)} fusion(f32[32,512,16,32,1,1]{1,3,2,5,4,0:T(8,128)} %bitcast.179, f32[2,3,32,2,512]{4,3,2,1,0:T(2,128)S(1)} %copy-done.1, f32[32,512]{1,0:T(8,128)S(1)} %fusion.74), kind=kOutput, calls=%fused_computation.31 | convolution fusion | flops 1208156160 | bytes 35192832 | tf_op jit(solution)/shard_map/lfsrn,snwt->lwftsr/dot_general | solution.py:64
  121.2 9.5 %copy.74 = f32[2,16,3,32,32,2]{1,5,4,3,2,0:T(2,128)} copy(f32[2,16,3,32,32,2]{3,2,1,5,0,4:T(4,128)} %convolution_bitcast_fusion.1) | data formatting | bytes 1572864 | tf_op jit(solution)/shard_map/lfsrn,snwt->lwftsr/transpose | solution.py:64
  130.7 5.4 copy.75
  136.1 8.4 %all-to-all-start = ((f32[2,16,6144]{2,0,1:T(2,128)}), f32[2,16,6144]{2,0,1:T(2,128)}, u32[]{:S(2)}, u32[]{:S(2)}) async-start(f32[2,16,6144]{2,0,1:T(2,128)} %copy.75), calls=%async_computation | async-start | bytes 1572864 | tf_op jit(solution)/shard_map/all_to_all | solution.py:73
  144.5 0.1 mul.312
  144.6 0.1 mul.325
  144.6 0.1 convert_element_type.67
  144.8 1.2 convert_element_type.69
  146.0 0.8 dynamic_slice.7
  146.7 10.7 %fusion.62 = (f32[16,32,1,1,1024]{4,1,0,3,2:T(8,128)S(1)}, f32[16,32,1,1,1024]{4,1,0,3,2:T(8,128)S(1)}, f32[16,32,1,1,1024]{4,1,0,2,3:T(8,128)S(1)}, f32[16,32,1...) fusion(s32[16,32]{1,0:T(8,128)S(1)} %mul.312), kind=kLoop, calls=%fused_computation.76 | loop fusion | flops 8388608 | bytes 12584960 | tf_op jit(solution)/shard_map/stack | solution.py:23
  157.4 2.6 fusion.14
  159.9 2.3 maximum_multiply_fusion.2
  162.3 2.0 all-to-all-done
  164.2 4.9 copy.76
  169.1 9.6 %copy.77 = f32[2,16,3,32,32,2]{4,3,1,5,2,0:T(8,128)} copy(f32[2,16,3,32,32,2]{1,5,4,3,2,0:T(2,128)} %bitcast.187) | data formatting | bytes 1572864 | tf_op jit(solution)/shard_map/reshape | solution.py:77
  178.7 9.6 %fusion.32 = f32[2,2,3,32,1024]{4,3,2,0,1:T(8,128)S(1)} fusion(f32[2,16,3,32,32,2]{4,3,1,5,2,0:T(8,128)} %copy.77, f32[16,32,2,1,1024]{4,1,0,2,3:T(8,128)} %maximum_multiply_fusion.2, f32[16,32,2,1,1024]{4,1,0,2,3:T(8,128)} %fusion.14), kind=kOutput, calls=%fused_computation.45 | convolution fusion | flops 4833935360 | bytes 10747904 | tf_op jit(solution)/shard_map/iwftsr,wsrkx->ikftx/dot_general | solution.py:78
  188.3 0.2 slice_bitcast_fusion
  188.5 0.6 multiply_reduce_fusion.2
  189.0 0.8 copy-done.8
  189.9 0.6 copy-done.9
  190.5 11.8 %fusion.24 = f32[2,16,3,32,32,2]{3,4,2,0,5,1:T(8,128)} fusion(f32[2,3,32,1024]{3,2,1,0:T(8,128)S(1)} %get-tuple-element.46, f32[2,3,32,1024]{3,2,1,0:T(8,128)S(1)} %get-tuple-element.45, f32[32]{0:T(128)S(1)} %dynamic_slice.7, f32[16,32,1,1024]{3,1,0,2:T(8,128)S(1)} %copy-done.8, f32[16,32,1,1024]{3,1,0,2:T(8,128)S(1)} %copy-done.9), kind=kOutput, calls=%fused_computation.40 | convolution fusion | flops 2418409472 | bytes 6553728 | tf_op jit(solution)/shard_map/iftx,wsrx->iwftsr/dot_general | solution.py:82
  202.2 10.9 %copy.79 = f32[2,16,3,32,32,2]{1,5,4,3,2,0:T(2,128)} copy(f32[2,16,3,32,32,2]{3,4,2,0,5,1:T(8,128)} %fusion.24) | data formatting | bytes 1572864 | tf_op jit(solution)/shard_map/iftx,wsrx->iwftsr/transpose | solution.py:82
  213.2 5.3 copy.80
  218.5 5.4 all-to-all-start.1
  224.6 18.5 %all-to-all-done.1 = f32[2,16,6144]{2,0,1:T(2,128)} async-done(((f32[2,16,6144]{2,0,1:T(2,128)}), f32[2,16,6144]{2,0,1:T(2,128)}, u32[]{:S(2)}, u32[]{:S(2)}) %all-to-all-start.1) | async-done | bytes 786464 | tf_op jit(solution)/shard_map/all_to_all | solution.py:83
  243.0 4.9 copy.81
  247.9 9.8 %copy.82 = f32[2,16,3,32,32,2]{3,2,1,5,0,4:T(4,128)} copy(f32[2,16,3,32,32,2]{1,5,4,3,2,0:T(2,128)} %bitcast.189) | data formatting | bytes 1572864 | tf_op jit(solution)/shard_map/reshape | solution.py:86
  257.7 37.0 %multiply_reduce_fusion.7 = (f32[]{:T(128)}, f32[2,3,32,2,512]{4,1,3,0,2:T(4,128)S(1)}) fusion(f32[2,3,32,2,512]{4,3,2,1,0:T(2,128)} %param.11, f32[]{:T(128)} %bitcast.177, f32[32,512]{1,0:T(8,128)S(1)} %fusion.74, f32[2,16,3,32,32,2]{3,2,1,5,0,4:T(4,128)} %copy.82, f32[32,512,16,32,1,1]{1,3,2,5,4,0:T(8,128)} %bitcast.180, ...), kind=kOutput, calls=%fused_computation.74 | convolution fusion | flops 1209729024 | bytes 36765704 | tf_op jit(solution)/shard_map/lwftsr,snwt->lfsrn/dot_general | solution.py:68
  294.7 1.0 copy-done
  295.7 75.5 %convolution_bitcast_fusion = f32[2,16,3,32,32,2]{3,2,1,5,0,4:T(4,128)} fusion(f32[32,512,16,32,1,1]{1,3,2,5,4,0:T(8,128)} %bitcast.181, f32[2,3,32,2,512]{4,1,3,0,2:T(4,128)S(1)} %get-tuple-element.44), kind=kOutput, calls=%fused_computation.30 | convolution fusion | flops 1207959552 | bytes 35127296 | tf_op jit(solution)/shard_map/lfsrn,snwt->lwftsr/dot_general | solution.py:64
  371.2 9.5 %copy.84 = f32[2,16,3,32,32,2]{1,5,4,3,2,0:T(2,128)} copy(f32[2,16,3,32,32,2]{3,2,1,5,0,4:T(4,128)} %convolution_bitcast_fusion) | data formatting | bytes 1572864 | tf_op jit(solution)/shard_map/lfsrn,snwt->lwftsr/transpose | solution.py:64
  380.7 4.5 copy.85
  385.2 25.1 %all_to_all.20 = f32[2,16,6144]{2,0,1:T(2,128)} all-to-all(f32[2,16,6144]{2,0,1:T(2,128)S(1)} %copy.85), channel_id=1, replica_groups=mesh['wave'=16,'field'=2] {'wave'}, dimensions={1} | all-to-all | bytes 1572864 | tf_op jit(solution)/shard_map/all_to_all | solution.py:94
  410.3 4.9 copy.86
  415.2 9.6 %copy.87 = f32[2,16,3,32,32,2]{4,3,1,5,2,0:T(8,128)} copy(f32[2,16,3,32,32,2]{1,5,4,3,2,0:T(2,128)} %bitcast.191) | data formatting | bytes 1572864 | tf_op jit(solution)/shard_map/reshape | solution.py:98
  424.7 7.9 %fusion.37 = f32[2,3,32,1024]{3,2,1,0:T(8,128)S(1)} fusion(f32[2,16,3,32,32,2]{4,3,1,5,2,0:T(8,128)} %copy.87, f32[32]{0:T(128)S(1)} %dynamic_slice.7, f32[16,32,1,1024]{3,1,0,2:T(8,128)} %get-tuple-element.41, f32[16,32,1,1024]{3,1,0,2:T(8,128)} %get-tuple-element.42), kind=kOutput, calls=%fused_computation.49 | convolution fusion | flops 2418212864 | bytes 5767296 | tf_op jit(solution)/shard_map/iwftsr,wsrx->iftx/dot_general | solution.py:99
  432.7 0.4 multiply_reduce_fusion.1
  433.1 1.7 copy-done.6
  434.8 20.4 %fusion.27 = f32[2,16,3,32,32,2]{3,4,2,0,5,1:T(8,128)S(1)} fusion(f32[2,1,3,32,1024]{4,3,1,2,0:T(8,128)S(1)} %bitcast.196, f32[2,1,3,32,1024]{4,3,1,2,0:T(8,128)S(1)} %bitcast.195, f32[16,32,2,1,1024]{4,1,0,2,3:T(8,128)S(1)} %copy-done.6, f32[16,32,2,1,1024]{4,1,0,2,3:T(8,128)S(1)} %copy-done.7), kind=kOutput, calls=%fused_computation.41 | convolution fusion | flops 4834328576 | bytes 10747904 | tf_op jit(solution)/shard_map/ikftx,wsrkx->iwftsr/dot_general | solution.py:103
  455.3 8.1 %copy.89 = f32[2,16,3,32,32,2]{1,5,4,3,2,0:T(2,128)} copy(f32[2,16,3,32,32,2]{3,4,2,0,5,1:T(8,128)S(1)} %fusion.27) | data formatting | bytes 1572864 | tf_op jit(solution)/shard_map/ikftx,wsrkx->iwftsr/transpose | solution.py:103
  463.4 5.3 copy.90
  468.8 3.8 all-to-all-start.3
  472.5 8.7 %convert_multiply_fusion = f32[20,2,3,32,2,512]{5,4,3,2,1,0:T(2,128)} fusion(bf16[20,2,3,32,2,512]{5,4,3,2,1,0:T(2,128)(2,1)} %param.13, f32[32,512]{1,0:T(8,128)S(1)} %fusion.74), kind=kLoop, calls=%fused_computation.8 | loop fusion | flops 7864320 | bytes 23658496 | tf_op jit(solution)/shard_map/mul | solution.py:88
  481.9 30.3 %reshape.276 = f32[20,196608]{1,0:T(8,128)} reshape(f32[20,2,3,32,2,512]{5,4,3,2,1,0:T(2,128)} %convert_multiply_fusion) | data formatting | bytes 31457280 | tf_op jit(solution)/shard_map/reshape | solution.py:88
  512.2 29.0 %dot_general.57 = f32[2,3,32,2,512,20]{4,3,2,1,0,5:T(2,128)} reshape(f32[196608,20]{0,1:T(8,128)} %bitcast.185) | data formatting | bytes 31457280 | tf_op jit(solution)/shard_map/dot_general | solution.py:144
  541.2 43.0 %fusion.47 = f32[20,20]{1,0:T(8,128)S(1)} fusion(f32[20,2,3,32,2,512]{5,4,3,2,1,0:T(2,128)} %convert_multiply_fusion), kind=kOutput, calls=%fused_computation.59 | convolution fusion | flops 943718400 | bytes 15730240 | tf_op jit(solution)/shard_map/dot_general | solution.py:117
  584.2 4.0 copy.91
  588.2 9.9 %copy.92 = f32[2,16,3,32,32,2]{3,2,1,5,0,4:T(4,128)} copy(f32[2,16,3,32,32,2]{1,5,4,3,2,0:T(2,128)} %bitcast.193) | data formatting | bytes 1572864 | tf_op jit(solution)/shard_map/reshape | solution.py:107
  598.1 36.4 %fusion.42 = f32[2,3,32,2,512]{4,1,3,0,2:T(4,128)S(1)} fusion(f32[2,3,32,2,512]{4,1,3,0,2:T(4,128)} %copy-done, f32[2,16,3,32,32,2]{3,2,1,5,0,4:T(4,128)} %copy.92, f32[32,512,16,32,1,1]{1,3,2,5,4,0:T(8,128)} %bitcast.182, f32[32,512]{1,0:T(8,128)S(1)} %fusion.74), kind=kOutput, calls=%fused_computation.54 | convolution fusion | flops 1208549376 | bytes 35979264 | tf_op jit(solution)/shard_map/lwftsr,snwt->lfsrn/dot_general | solution.py:68
  634.6 1.9 multiply_reduce_fusion.5
  636.5 22.9 %fusion.50 = f32[20]{0:T(128)S(1)} fusion(f32[20,2,3,32,2,512]{5,4,3,2,1,0:T(2,128)S(1)} %bitcast.184, f32[2,3,32,2,512,1]{4,1,3,0,2,5:T(4,128)S(1)} %bitcast.194), kind=kOutput, calls=%fused_computation.60 | convolution fusion | flops 47185920 | bytes 16515152 | tf_op jit(solution)/shard_map/dot_general | solution.py:92
  659.4 22.9 %fusion.53 = f32[20]{0:T(128)S(1)} fusion(f32[20,2,3,32,2,512]{5,4,3,2,1,0:T(2,128)S(1)} %bitcast.184, f32[2,3,32,2,512,1]{4,1,3,0,2,5:T(4,128)S(1)} %get-tuple-element.36), kind=kOutput, calls=%fused_computation.61 | convolution fusion | flops 47185920 | bytes 16515152 | tf_op jit(solution)/shard_map/dot_general | solution.py:92
  682.3 41.9 %all-reduce = (f32[]{:T(128)}, f32[20]{0:T(128)S(1)}, f32[20]{0:T(128)S(1)}, f32[]{:T(128)}, f32[]{:T(128)}, /*index=5*/f32[]{:T(128)}, f32[20,20]{1,0:T(8,128)S(1)}) all-reduce(f32[]{:T(128)} %get-tuple-element.43, f32[20]{0:T(128)S(1)} %fusion.53, f32[20]{0:T(128)S(1)} %fusion.50, ...), channel_id=1, replica_groups=mesh['wave'=16,'field'=2] {'wave','field'}, use_global_device_ids=true, to_apply=%region_3.4 | all-reduce | flops 444 | bytes 3552 | tf_op jit(solution)/shard_map/psum | solution.py:109
  724.9 1.5 broadcast_divide_fusion
  727.8 0.6 multiply_reduce_fusion.8
  728.4 0.7 fusion.71
  731.2 24.4 %fusion.6 = f32[1,2,3,32,2,512]{5,0,4,3,2,1:T(1,128)S(1)} fusion(f32[2,3,32,2,512,20]{4,3,2,1,0,5:T(2,128)} %dot_general.57, f32[20]{0:T(128)S(1)} %get-tuple-element.33), kind=kOutput, calls=%fused_computation.6 | convolution fusion | flops 47185920 | bytes 16515152 | tf_op jit(solution)/shard_map/dot_general | solution.py:144
  755.6 1.3 fusion.65
  756.9 1.3 copy.96
  758.2 1.3 copy.95
  759.5 0.6 pad_maximum_fusion.2
  (33 shorter events, 0.1 us)
Async XLA Ops:
  1.5 33.4 %copy-start.1 = (f32[2,3,32,2,512]{4,3,2,1,0:T(2,128)S(1)}, f32[2,3,32,2,512]{4,3,2,1,0:T(2,128)}, u32[]{:S(2)}) copy-start(f32[2,3,32,2,512]{4,3,2,1,0:T(2,128)} %param.10) | copy-start | bytes 2359300
  130.7 13.8 %copy-start.11 = (s32[512]{0:T(512)S(1)}, s32[512]{0:T(512)}, u32[]{:S(2)}) copy-start(s32[512]{0:T(512)} %param.15) | copy-start | bytes 6148
  130.7 13.9 %copy-start.10 = (bf16[3,3,32,1024]{3,2,1,0:T(8,128)(2,1)S(1)}, bf16[3,3,32,1024]{3,2,1,0:T(8,128)(2,1)}, u32[]{:S(2)}) copy-start(bf16[3,3,32,1024]{3,2,1,0:T(8,128)(2,1)} %param.18) | copy-start | bytes 1769476
  136.1 28.1 %all-to-all-start = ((f32[2,16,6144]{2,0,1:T(2,128)}), f32[2,16,6144]{2,0,1:T(2,128)}, u32[]{:S(2)}, u32[]{:S(2)}) async-start(f32[2,16,6144]{2,0,1:T(2,128)} %copy.75), calls=%async_computation | async-start | bytes 1572864 | tf_op jit(solution)/shard_map/all_to_all | solution.py:73
  188.3 1.6 copy-start.8
  188.3 2.2 copy-start.9
  218.5 24.5 %all-to-all-start.1 = ((f32[2,16,6144]{2,0,1:T(2,128)}), f32[2,16,6144]{2,0,1:T(2,128)}, u32[]{:S(2)}, u32[]{:S(2)}) async-start(f32[2,16,6144]{2,0,1:T(2,128)} %copy.80), calls=%async_computation.1 | async-start | bytes 1572864 | tf_op jit(solution)/shard_map/all_to_all | solution.py:83
  294.7 1.0 copy-start
  424.7 8.4 %copy-start.7 = (f32[16,32,2,1,1024]{4,1,0,2,3:T(8,128)S(1)}, f32[16,32,2,1,1024]{4,1,0,2,3:T(8,128)}, u32[]{:S(2)}) copy-start(f32[16,32,2,1,1024]{4,1,0,2,3:T(8,128)} %fusion.14) | copy-start | bytes 12582916
  432.7 2.2 copy-start.6
  468.8 115.4 %all-to-all-start.3 = ((f32[2,16,6144]{2,0,1:T(2,128)}), f32[2,16,6144]{2,0,1:T(2,128)S(1)}, u32[]{:S(2)}, u32[]{:S(2)}) async-start(f32[2,16,6144]{2,0,1:T(2,128)} %copy.90), calls=%async_computation.3 | async-start | bytes 1572864 | tf_op jit(solution)/shard_map/all_to_all | solution.py:104
  588.2 48.3 %slice-start = ((s8[15728640]{0:T(1024)(128)(4,1)}), s8[3145728]{0:T(1024)(128)(4,1)S(1)}, s32[]{:S(2)}) async-start(s8[15728640]{0:T(1024)(128)(4,1)} %bitcast.183), calls=%async_computation.4 | async-start | bytes 6291456
  598.1 36.4 %copy-start.2 = (f32[2,3,32,2,512]{4,3,2,1,0:T(2,128)S(1)}, f32[2,3,32,2,512]{4,3,2,1,0:T(2,128)}, u32[]{:S(2)}) copy-start(f32[2,3,32,2,512]{4,3,2,1,0:T(2,128)} %param.10) | copy-start | bytes 2359300
  598.1 38.4 %slice-start.1 = ((s8[15728640]{0:T(1024)(128)(4,1)}), s8[4194304]{0:T(1024)(128)(4,1)S(1)}, s32[]{:S(2)}) async-start(s8[15728640]{0:T(1024)(128)(4,1)} %bitcast.183), calls=%async_computation.5 | async-start | bytes 8388608
  598.1 38.4 %slice-start.2 = ((s8[15728640]{0:T(1024)(128)(4,1)}), s8[4194304]{0:T(1024)(128)(4,1)S(1)}, s32[]{:S(2)}) async-start(s8[15728640]{0:T(1024)(128)(4,1)} %bitcast.183), calls=%async_computation.6 | async-start | bytes 8388608
  598.1 38.4 %slice-start.3 = ((s8[15728640]{0:T(1024)(128)(4,1)}), s8[4194304]{0:T(1024)(128)(4,1)S(1)}, s32[]{:S(2)}) async-start(s8[15728640]{0:T(1024)(128)(4,1)} %bitcast.183), calls=%async_computation.7 | async-start | bytes 8388608
  634.6 24.8 %copy-start.4 = (f32[2,3,32,2,512]{4,1,3,0,2:T(4,128)}, f32[2,3,32,2,512]{4,1,3,0,2:T(4,128)S(1)}, u32[]{:S(2)}) copy-start(f32[2,3,32,2,512]{4,1,3,0,2:T(4,128)S(1)} %fusion.42) | copy-start | bytes 2359300
  728.4 27.2 %copy-start.12 = (f32[20]{0:T(128)}, f32[20]{0:T(128)S(1)}, u32[]{:S(2)}) copy-start(f32[20]{0:T(128)S(1)} %get-tuple-element.33) | copy-start | bytes 244
  731.1 24.5 %copy-start.3 = (f32[2,3,32,2,512]{4,3,2,1,0:T(2,128)S(1)}, f32[2,3,32,2,512]{4,3,2,1,0:T(2,128)}, u32[]{:S(2)}) copy-start(f32[2,3,32,2,512]{4,3,2,1,0:T(2,128)} %param.10) | copy-start | bytes 2359300
  731.2 24.5 %copy-start.5 = (f32[2,3,32,2,512]{4,1,3,0,2:T(4,128)S(1)}, f32[2,3,32,2,512]{4,1,3,0,2:T(4,128)}, u32[]{:S(2)}) copy-start(f32[2,3,32,2,512]{4,1,3,0,2:T(4,128)} %copy-done.4) | copy-start | bytes 2359300
where the time goes:
time: 773 us; the launch traced here: 761 us
  matrix products  399 us (52%)
  local copies, waits for them, and re-layouts  217 us (28%)
  blocking collectives  67.1 us (9%)
  other arithmetic  32.5 us (4%)
  waiting for transfers between devices  20.4 us (3%)
  starting transfers between devices  17.6 us (2%)
    dot_general x2, matrix products, to_latitudes(): jnp.einsum('lfsrn,snwt->lwftsr', spectral, blocked, precision=highest)  162 us
    dot_general x2, matrix products, to_degrees(): jnp.einsum('lwftsr,snwt->lfsrn', gathered, blocked, precision=highest)  73.4 us
    dot_general x2, matrix products, project(): return jnp.dot(kept_live, vector.reshape(-1), precision=highest)  45.8 us
    dot_general x1, matrix products, body(): jnp.dot(kept_live, kept_live.T, precision=highest)  43 us
    psum x1, blocking collectives, body(): lax.psum((jnp.sum(residual_left * residual_left), jnp.sum(adjoint_raw * a...  41.9 us
    unnamed x37, local copies, waits for them, and re-layouts  40.2 us
    reshape x1, local copies, waits for them, and re-layouts, body(): (kept_vectors.astype(jnp.float32) * wide_mask[None]).reshape(keep_count, -1)  30.3 us
    dot_general x1, local copies, waits for them, and re-layouts, body(): jnp.dot(correlations, kept_live, precision=highest)  29 us
  transfers between devices with their start and end apart: 3, of which 2 were waited for; matrix products, arithmetic and copies ran while one was open for 17% of the time, Pallas kernels for 0%

commit v1 on v0

--- a/solution.py
+++ b/solution.py
@@ -7,6 +7,10 @@
 time_step = 0.5
 epsilon = 1e-06
 highest = lax.Precision.HIGHEST
+
+
+def attach_rails(local_array):
+    return lax.psum(lax.psum(local_array, "field"), "wave")
 
 
 def fourier_tables(wave_table, longitudes, wave_count):
@@ -106,7 +110,7 @@
     )
     gathered = returned.reshape(item_count, groups, fields, lat_dev, waves_dev, 2)
     adjoint_raw = residual_left + time_step * to_degrees(gathered)
-    totals = lax.psum(
+    totals = attach_rails(
         (
             jnp.sum(residual_left * residual_left),
             jnp.sum(adjoint_raw * adjoint_raw),
@@ -115,8 +119,7 @@
             project(adjoint_raw),
             project(right_live),
             jnp.dot(kept_live, kept_live.T, precision=highest),
-        ),
-        ("wave", "field"),
+        )
     )
     left_square, image_square, image_cross, right_square, kept_image, kept_right, gram_matrix = [
         summed / entries for summed in totals

time: 773 us -> 814 us (1.053)
  blocking collectives: 67.1 us -> 107 us
    psum x1 -> x2, blocking collectives: 41.9 us -> 81.7 us  [attach_rails(): return lax.psum(lax.psum(local_array, 'field'), 'wave')]
  transfers between devices with their start and end apart: 3 -> 3, of which waited for: 2 -> 2; matrix products, arithmetic and copies ran while one was open for 17% -> 16% of each run, Pallas kernels for 0% -> 0%
where the time goes in v1:
time: 814 us; the launch traced here: 801 us
  matrix products  400 us (49%)
  local copies, waits for them, and re-layouts  217 us (27%)
  blocking collectives  107 us (13%)
  other arithmetic  32.6 us (4%)
  waiting for transfers between devices  20.4 us (3%)
  starting transfers between devices  17.6 us (2%)
    dot_general x2, matrix products, to_latitudes(): jnp.einsum('lfsrn,snwt->lwftsr', spectral, blocked, precision=highest)  162 us
    psum x2, blocking collectives, attach_rails(): return lax.psum(lax.psum(local_array, 'field'), 'wave')  81.7 us
    dot_general x2, matrix products, to_degrees(): jnp.einsum('lwftsr,snwt->lfsrn', gathered, blocked, precision=highest)  73.4 us
    dot_general x2, matrix products, project(): return jnp.dot(kept_live, vector.reshape(-1), precision=highest)  45.8 us
    dot_general x1, matrix products, body(): jnp.dot(kept_live, kept_live.T, precision=highest)  43.9 us
    unnamed x37, local copies, waits for them, and re-layouts  40.2 us
    reshape x1, local copies, waits for them, and re-layouts, body(): (kept_vectors.astype(jnp.float32) * wide_mask[None]).reshape(keep_count, -1)  30.4 us
    dot_general x1, local copies, waits for them, and re-layouts, body(): jnp.dot(correlations, kept_live, precision=highest)  29 us
  transfers between devices with their start and end apart: 3, of which 2 were waited for; matrix products, arithmetic and copies ran while one was open for 16% of the time, Pallas kernels for 0%

profile of v1, /device:TPU:0, one launch (start us, length us, event | category | flops | bytes accessed | tf_op | source)
XLA Modules:
  0.0 801.1 jit_solution(1283704664223622971)
XLA Ops:
  0.6 0.8 dynamic_slice.6
  1.4 0.1 fusion.74
  1.5 33.4 %copy.73 = f32[32,512,512]{1,2,0:T(8,128)} copy(f32[32,512,512]{2,1,0:T(8,128)} %param.16) | data formatting | bytes 67108864 | tf_op args[6]
  34.9 86.3 %convolution_bitcast_fusion.1 = f32[2,16,3,32,32,2]{3,2,1,5,0,4:T(4,128)} fusion(f32[32,512,16,32,1,1]{1,3,2,5,4,0:T(8,128)} %bitcast.179, f32[2,3,32,2,512]{4,3,2,1,0:T(2,128)S(1)} %copy-done.1, f32[32,512]{1,0:T(8,128)S(1)} %fusion.74), kind=kOutput, calls=%fused_computation.31 | convolution fusion | flops 1208156160 | bytes 35192832 | tf_op jit(solution)/shard_map/lfsrn,snwt->lwftsr/dot_general | solution.py:68
  121.2 9.5 %copy.74 = f32[2,16,3,32,32,2]{1,5,4,3,2,0:T(2,128)} copy(f32[2,16,3,32,32,2]{3,2,1,5,0,4:T(4,128)} %convolution_bitcast_fusion.1) | data formatting | bytes 1572864 | tf_op jit(solution)/shard_map/lfsrn,snwt->lwftsr/transpose | solution.py:68
  130.7 5.4 copy.75
  136.1 8.4 %all-to-all-start = ((f32[2,16,6144]{2,0,1:T(2,128)}), f32[2,16,6144]{2,0,1:T(2,128)}, u32[]{:S(2)}, u32[]{:S(2)}) async-start(f32[2,16,6144]{2,0,1:T(2,128)} %copy.75), calls=%async_computation | async-start | bytes 1572864 | tf_op jit(solution)/shard_map/all_to_all | solution.py:77
  144.6 0.1 mul.325
  144.6 0.1 convert_element_type.67
  144.8 1.2 convert_element_type.69
  146.0 0.8 dynamic_slice.7
  146.7 10.7 %fusion.62 = (f32[16,32,1,1,1024]{4,1,0,3,2:T(8,128)S(1)}, f32[16,32,1,1,1024]{4,1,0,3,2:T(8,128)S(1)}, f32[16,32,1,1,1024]{4,1,0,2,3:T(8,128)S(1)}, f32[16,32,1...) fusion(s32[16,32]{1,0:T(8,128)S(1)} %mul.312), kind=kLoop, calls=%fused_computation.76 | loop fusion | flops 8388608 | bytes 12584960 | tf_op jit(solution)/shard_map/stack | solution.py:27
  157.4 2.6 fusion.14
  160.0 2.3 maximum_multiply_fusion.2
  162.3 1.9 all-to-all-done
  164.2 4.9 copy.76
  169.1 9.5 %copy.77 = f32[2,16,3,32,32,2]{4,3,1,5,2,0:T(8,128)} copy(f32[2,16,3,32,32,2]{1,5,4,3,2,0:T(2,128)} %bitcast.187) | data formatting | bytes 1572864 | tf_op jit(solution)/shard_map/reshape | solution.py:81
  178.6 9.6 %fusion.32 = f32[2,2,3,32,1024]{4,3,2,0,1:T(8,128)S(1)} fusion(f32[2,16,3,32,32,2]{4,3,1,5,2,0:T(8,128)} %copy.77, f32[16,32,2,1,1024]{4,1,0,2,3:T(8,128)} %maximum_multiply_fusion.2, f32[16,32,2,1,1024]{4,1,0,2,3:T(8,128)} %fusion.14), kind=kOutput, calls=%fused_computation.45 | convolution fusion | flops 4833935360 | bytes 10747904 | tf_op jit(solution)/shard_map/iwftsr,wsrkx->ikftx/dot_general | solution.py:82
  188.2 0.2 slice_bitcast_fusion
  188.4 0.6 multiply_reduce_fusion.2
  189.0 0.8 copy-done.8
  189.8 0.6 copy-done.9
  190.4 11.7 %fusion.24 = f32[2,16,3,32,32,2]{3,4,2,0,5,1:T(8,128)} fusion(f32[2,3,32,1024]{3,2,1,0:T(8,128)S(1)} %get-tuple-element.53, f32[2,3,32,1024]{3,2,1,0:T(8,128)S(1)} %get-tuple-element.52, f32[32]{0:T(128)S(1)} %dynamic_slice.7, f32[16,32,1,1024]{3,1,0,2:T(8,128)S(1)} %copy-done.8, f32[16,32,1,1024]{3,1,0,2:T(8,128)S(1)} %copy-done.9), kind=kOutput, calls=%fused_computation.40 | convolution fusion | flops 2418409472 | bytes 6553728 | tf_op jit(solution)/shard_map/iftx,wsrx->iwftsr/dot_general | solution.py:86
  202.2 11.0 %copy.79 = f32[2,16,3,32,32,2]{1,5,4,3,2,0:T(2,128)} copy(f32[2,16,3,32,32,2]{3,4,2,0,5,1:T(8,128)} %fusion.24) | data formatting | bytes 1572864 | tf_op jit(solution)/shard_map/iftx,wsrx->iwftsr/transpose | solution.py:86
  213.1 5.3 copy.80
  218.4 5.4 all-to-all-start.1
  224.5 18.5 %all-to-all-done.1 = f32[2,16,6144]{2,0,1:T(2,128)} async-done(((f32[2,16,6144]{2,0,1:T(2,128)}), f32[2,16,6144]{2,0,1:T(2,128)}, u32[]{:S(2)}, u32[]{:S(2)}) %all-to-all-start.1) | async-done | bytes 786464 | tf_op jit(solution)/shard_map/all_to_all | solution.py:87
  243.0 4.9 copy.81
  247.9 9.8 %copy.82 = f32[2,16,3,32,32,2]{3,2,1,5,0,4:T(4,128)} copy(f32[2,16,3,32,32,2]{1,5,4,3,2,0:T(2,128)} %bitcast.189) | data formatting | bytes 1572864 | tf_op jit(solution)/shard_map/reshape | solution.py:90
  257.6 37.0 %multiply_reduce_fusion.7 = (f32[]{:T(128)}, f32[2,3,32,2,512]{4,1,3,0,2:T(4,128)S(1)}) fusion(f32[2,3,32,2,512]{4,3,2,1,0:T(2,128)} %param.11, f32[]{:T(128)} %bitcast.177, f32[32,512]{1,0:T(8,128)S(1)} %fusion.74, f32[2,16,3,32,32,2]{3,2,1,5,0,4:T(4,128)} %copy.82, f32[32,512,16,32,1,1]{1,3,2,5,4,0:T(8,128)} %bitcast.180, ...), kind=kOutput, calls=%fused_computation.74 | convolution fusion | flops 1209729024 | bytes 36765704 | tf_op jit(solution)/shard_map/lwftsr,snwt->lfsrn/dot_general | solution.py:72
  294.7 1.0 copy-done
  295.6 75.5 %convolution_bitcast_fusion = f32[2,16,3,32,32,2]{3,2,1,5,0,4:T(4,128)} fusion(f32[32,512,16,32,1,1]{1,3,2,5,4,0:T(8,128)} %bitcast.181, f32[2,3,32,2,512]{4,1,3,0,2:T(4,128)S(1)} %get-tuple-element.51), kind=kOutput, calls=%fused_computation.30 | convolution fusion | flops 1207959552 | bytes 35127296 | tf_op jit(solution)/shard_map/lfsrn,snwt->lwftsr/dot_general | solution.py:68
  371.1 9.5 %copy.84 = f32[2,16,3,32,32,2]{1,5,4,3,2,0:T(2,128)} copy(f32[2,16,3,32,32,2]{3,2,1,5,0,4:T(4,128)} %convolution_bitcast_fusion) | data formatting | bytes 1572864 | tf_op jit(solution)/shard_map/lfsrn,snwt->lwftsr/transpose | solution.py:68
  380.6 4.5 copy.85
  385.1 25.1 %all_to_all.20 = f32[2,16,6144]{2,0,1:T(2,128)} all-to-all(f32[2,16,6144]{2,0,1:T(2,128)S(1)} %copy.85), channel_id=1, replica_groups=mesh['wave'=16,'field'=2] {'wave'}, dimensions={1} | all-to-all | bytes 1572864 | tf_op jit(solution)/shard_map/all_to_all | solution.py:98
  410.2 4.9 copy.86
  415.1 9.5 %copy.87 = f32[2,16,3,32,32,2]{4,3,1,5,2,0:T(8,128)} copy(f32[2,16,3,32,32,2]{1,5,4,3,2,0:T(2,128)} %bitcast.191) | data formatting | bytes 1572864 | tf_op jit(solution)/shard_map/reshape | solution.py:102
  424.6 7.9 fusion.37
  432.6 0.4 multiply_reduce_fusion.1
  433.0 1.7 copy-done.6
  434.8 20.4 %fusion.27 = f32[2,16,3,32,32,2]{3,4,2,0,5,1:T(8,128)S(1)} fusion(f32[2,1,3,32,1024]{4,3,1,2,0:T(8,128)S(1)} %bitcast.196, f32[2,1,3,32,1024]{4,3,1,2,0:T(8,128)S(1)} %bitcast.195, f32[16,32,2,1,1024]{4,1,0,2,3:T(8,128)S(1)} %copy-done.6, f32[16,32,2,1,1024]{4,1,0,2,3:T(8,128)S(1)} %copy-done.7), kind=kOutput, calls=%fused_computation.41 | convolution fusion | flops 4834328576 | bytes 10747904 | tf_op jit(solution)/shard_map/ikftx,wsrkx->iwftsr/dot_general | solution.py:107
  455.2 8.2 %copy.89 = f32[2,16,3,32,32,2]{1,5,4,3,2,0:T(2,128)} copy(f32[2,16,3,32,32,2]{3,4,2,0,5,1:T(8,128)S(1)} %fusion.27) | data formatting | bytes 1572864 | tf_op jit(solution)/shard_map/ikftx,wsrkx->iwftsr/transpose | solution.py:107
  463.4 5.3 copy.90
  468.7 3.8 all-to-all-start.3
  472.5 8.7 %convert_multiply_fusion = f32[20,2,3,32,2,512]{5,4,3,2,1,0:T(2,128)} fusion(bf16[20,2,3,32,2,512]{5,4,3,2,1,0:T(2,128)(2,1)} %param.13, f32[32,512]{1,0:T(8,128)S(1)} %fusion.74), kind=kLoop, calls=%fused_computation.8 | loop fusion | flops 7864320 | bytes 23658496 | tf_op jit(solution)/shard_map/mul | solution.py:92
  481.8 30.4 %reshape.276 = f32[20,196608]{1,0:T(8,128)} reshape(f32[20,2,3,32,2,512]{5,4,3,2,1,0:T(2,128)} %convert_multiply_fusion) | data formatting | bytes 31457280 | tf_op jit(solution)/shard_map/reshape | solution.py:92
  512.2 29.0 %dot_general.57 = f32[2,3,32,2,512,20]{4,3,2,1,0,5:T(2,128)} reshape(f32[196608,20]{0,1:T(8,128)} %bitcast.185) | data formatting | bytes 31457280 | tf_op jit(solution)/shard_map/dot_general | solution.py:147
  541.2 43.9 %fusion.47 = f32[20,20]{1,0:T(8,128)S(1)} fusion(f32[20,2,3,32,2,512]{5,4,3,2,1,0:T(2,128)} %convert_multiply_fusion), kind=kOutput, calls=%fused_computation.59 | convolution fusion | flops 943718400 | bytes 15730240 | tf_op jit(solution)/shard_map/dot_general | solution.py:121
  585.1 4.0 copy.91
  589.0 9.9 %copy.92 = f32[2,16,3,32,32,2]{3,2,1,5,0,4:T(4,128)} copy(f32[2,16,3,32,32,2]{1,5,4,3,2,0:T(2,128)} %bitcast.193) | data formatting | bytes 1572864 | tf_op jit(solution)/shard_map/reshape | solution.py:111
  599.0 36.4 %fusion.42 = f32[2,3,32,2,512]{4,1,3,0,2:T(4,128)S(1)} fusion(f32[2,3,32,2,512]{4,1,3,0,2:T(4,128)} %copy-done, f32[2,16,3,32,32,2]{3,2,1,5,0,4:T(4,128)} %copy.92, f32[32,512,16,32,1,1]{1,3,2,5,4,0:T(8,128)} %bitcast.182, f32[32,512]{1,0:T(8,128)S(1)} %fusion.74), kind=kOutput, calls=%fused_computation.54 | convolution fusion | flops 1208549376 | bytes 35979264 | tf_op jit(solution)/shard_map/lwftsr,snwt->lfsrn/dot_general | solution.py:72
  635.4 1.9 multiply_reduce_fusion.5
  637.3 22.9 %fusion.50 = f32[20]{0:T(128)S(1)} fusion(f32[20,2,3,32,2,512]{5,4,3,2,1,0:T(2,128)S(1)} %bitcast.184, f32[2,3,32,2,512,1]{4,1,3,0,2,5:T(4,128)S(1)} %bitcast.194), kind=kOutput, calls=%fused_computation.60 | convolution fusion | flops 47185920 | bytes 16515152 | tf_op jit(solution)/shard_map/dot_general | solution.py:96
  660.2 22.9 %fusion.53 = f32[20]{0:T(128)S(1)} fusion(f32[20,2,3,32,2,512]{5,4,3,2,1,0:T(2,128)S(1)} %bitcast.184, f32[2,3,32,2,512,1]{4,1,3,0,2,5:T(4,128)S(1)} %get-tuple-element.43), kind=kOutput, calls=%fused_computation.61 | convolution fusion | flops 47185920 | bytes 16515152 | tf_op jit(solution)/shard_map/dot_general | solution.py:96
  683.1 4.5 all-reduce.1
  687.6 77.2 %all-reduce = (f32[]{:T(128)}, f32[20]{0:T(128)S(1)}, f32[20]{0:T(128)S(1)}, f32[]{:T(128)}, f32[]{:T(128)}, /*index=5*/f32[]{:T(128)}, f32[20,20]{1,0:T(8,128)S(1)}) all-reduce(f32[]{:T(128)} %get-tuple-element.32, f32[20]{0:T(128)S(1)} %get-tuple-element.33, ...), channel_id=1, replica_groups=mesh['wave'=16,'field'=2] {'wave'}, use_global_device_ids=true, to_apply=%region_4.5 | all-reduce | flops 444 | bytes 3552 | tf_op jit(solution)/shard_map/psum | solution.py:13
  765.5 1.5 broadcast_divide_fusion
  768.3 0.6 multiply_reduce_fusion.8
  769.0 0.7 fusion.71
  771.7 24.4 %fusion.6 = f32[1,2,3,32,2,512]{5,0,4,3,2,1:T(1,128)S(1)} fusion(f32[2,3,32,2,512,20]{4,3,2,1,0,5:T(2,128)} %dot_general.57, f32[20]{0:T(128)S(1)} %get-tuple-element.40), kind=kOutput, calls=%fused_computation.6 | convolution fusion | flops 47185920 | bytes 16515152 | tf_op jit(solution)/shard_map/dot_general | solution.py:147
  796.2 1.3 fusion.65
  797.5 1.3 copy.96
  798.8 1.3 copy.95
  800.1 0.6 pad_maximum_fusion.2
  (34 shorter events, 0.1 us)
Async XLA Ops:
  1.5 33.4 %copy-start.1 = (f32[2,3,32,2,512]{4,3,2,1,0:T(2,128)S(1)}, f32[2,3,32,2,512]{4,3,2,1,0:T(2,128)}, u32[]{:S(2)}) copy-start(f32[2,3,32,2,512]{4,3,2,1,0:T(2,128)} %param.10) | copy-start | bytes 2359300
  130.7 13.8 %copy-start.11 = (s32[512]{0:T(512)S(1)}, s32[512]{0:T(512)}, u32[]{:S(2)}) copy-start(s32[512]{0:T(512)} %param.15) | copy-start | bytes 6148
  130.7 13.9 %copy-start.10 = (bf16[3,3,32,1024]{3,2,1,0:T(8,128)(2,1)S(1)}, bf16[3,3,32,1024]{3,2,1,0:T(8,128)(2,1)}, u32[]{:S(2)}) copy-start(bf16[3,3,32,1024]{3,2,1,0:T(8,128)(2,1)} %param.18) | copy-start | bytes 1769476
  136.1 28.1 %all-to-all-start = ((f32[2,16,6144]{2,0,1:T(2,128)}), f32[2,16,6144]{2,0,1:T(2,128)}, u32[]{:S(2)}, u32[]{:S(2)}) async-start(f32[2,16,6144]{2,0,1:T(2,128)} %copy.75), calls=%async_computation | async-start | bytes 1572864 | tf_op jit(solution)/shard_map/all_to_all | solution.py:77
  188.2 1.6 copy-start.8
  188.2 2.2 copy-start.9
  218.4 24.6 %all-to-all-start.1 = ((f32[2,16,6144]{2,0,1:T(2,128)}), f32[2,16,6144]{2,0,1:T(2,128)}, u32[]{:S(2)}, u32[]{:S(2)}) async-start(f32[2,16,6144]{2,0,1:T(2,128)} %copy.80), calls=%async_computation.1 | async-start | bytes 1572864 | tf_op jit(solution)/shard_map/all_to_all | solution.py:87
  294.6 1.0 copy-start
  424.6 8.4 %copy-start.7 = (f32[16,32,2,1,1024]{4,1,0,2,3:T(8,128)S(1)}, f32[16,32,2,1,1024]{4,1,0,2,3:T(8,128)}, u32[]{:S(2)}) copy-start(f32[16,32,2,1,1024]{4,1,0,2,3:T(8,128)} %fusion.14) | copy-start | bytes 12582916
  432.6 2.2 copy-start.6
  468.7 116.3 %all-to-all-start.3 = ((f32[2,16,6144]{2,0,1:T(2,128)}), f32[2,16,6144]{2,0,1:T(2,128)S(1)}, u32[]{:S(2)}, u32[]{:S(2)}) async-start(f32[2,16,6144]{2,0,1:T(2,128)} %copy.90), calls=%async_computation.3 | async-start | bytes 1572864 | tf_op jit(solution)/shard_map/all_to_all | solution.py:108
  589.0 48.3 %slice-start = ((s8[15728640]{0:T(1024)(128)(4,1)}), s8[3145728]{0:T(1024)(128)(4,1)S(1)}, s32[]{:S(2)}) async-start(s8[15728640]{0:T(1024)(128)(4,1)} %bitcast.183), calls=%async_computation.4 | async-start | bytes 6291456
  599.0 36.4 %copy-start.2 = (f32[2,3,32,2,512]{4,3,2,1,0:T(2,128)S(1)}, f32[2,3,32,2,512]{4,3,2,1,0:T(2,128)}, u32[]{:S(2)}) copy-start(f32[2,3,32,2,512]{4,3,2,1,0:T(2,128)} %param.10) | copy-start | bytes 2359300
  599.0 38.4 %slice-start.1 = ((s8[15728640]{0:T(1024)(128)(4,1)}), s8[4194304]{0:T(1024)(128)(4,1)S(1)}, s32[]{:S(2)}) async-start(s8[15728640]{0:T(1024)(128)(4,1)} %bitcast.183), calls=%async_computation.5 | async-start | bytes 8388608
  599.0 38.4 %slice-start.2 = ((s8[15728640]{0:T(1024)(128)(4,1)}), s8[4194304]{0:T(1024)(128)(4,1)S(1)}, s32[]{:S(2)}) async-start(s8[15728640]{0:T(1024)(128)(4,1)} %bitcast.183), calls=%async_computation.6 | async-start | bytes 8388608
  599.0 38.4 %slice-start.3 = ((s8[15728640]{0:T(1024)(128)(4,1)}), s8[4194304]{0:T(1024)(128)(4,1)S(1)}, s32[]{:S(2)}) async-start(s8[15728640]{0:T(1024)(128)(4,1)} %bitcast.183), calls=%async_computation.7 | async-start | bytes 8388608
  635.4 24.8 %copy-start.4 = (f32[2,3,32,2,512]{4,1,3,0,2:T(4,128)}, f32[2,3,32,2,512]{4,1,3,0,2:T(4,128)S(1)}, u32[]{:S(2)}) copy-start(f32[2,3,32,2,512]{4,1,3,0,2:T(4,128)S(1)} %fusion.42) | copy-start | bytes 2359300
  769.0 27.2 %copy-start.12 = (f32[20]{0:T(128)}, f32[20]{0:T(128)S(1)}, u32[]{:S(2)}) copy-start(f32[20]{0:T(128)S(1)} %get-tuple-element.40) | copy-start | bytes 244
  771.7 24.5 %copy-start.3 = (f32[2,3,32,2,512]{4,3,2,1,0:T(2,128)S(1)}, f32[2,3,32,2,512]{4,3,2,1,0:T(2,128)}, u32[]{:S(2)}) copy-start(f32[2,3,32,2,512]{4,3,2,1,0:T(2,128)} %param.10) | copy-start | bytes 2359300
  771.7 24.5 %copy-start.5 = (f32[2,3,32,2,512]{4,1,3,0,2:T(4,128)S(1)}, f32[2,3,32,2,512]{4,1,3,0,2:T(4,128)}, u32[]{:S(2)}) copy-start(f32[2,3,32,2,512]{4,1,3,0,2:T(4,128)} %copy-done.4) | copy-start | bytes 2359300
